TPU v7x, 256 devices: a whole 4x4x8 slice. The times are simulated.
256 devices in a mesh: tp: 16 (over x_lo, y, core), grp: 16 (over z, x_hi).
Axes of the slice: x: 4 (x_hi: 2, x_lo: 2; x = x_hi * 2 + x_lo), y: 4, z: 8, core: 2. Of those that a mesh axis runs over, the one named last changes fastest.
Arguments:
- resid_in: bfloat16 [1024, 8192], P('grp', 'tp'), may hold values from -6 to 6
- queries: bfloat16 [1024, 4096], P('grp', 'tp')
- kv_cache: bfloat16 [2, 1024, 16, 128, 128], P(None, 'grp', 'tp'), as said below
- new_kv: bfloat16 [2, 1024, 4, 128], P(None, 'grp')
- lengths: int32 [1024], P('grp'), may hold values from 1 to 128, 65536 in all
- out_weight: bfloat16 [4096, 8192], P('tp'), may hold values from -0.09375 to 0.09375
- enc_weight: bfloat16 [8192, 32768], P('tp', 'grp'), may hold values from -0.0625 to 0.0625
- enc_bias: float32 [32768], P('grp'), may hold values from -1 to 0.5
- dec_weight: bfloat16 [32768, 8192], P('grp', 'tp'), may hold values from -0.75 to 0.75
- clamp_ids: int32 [1024, 4], P('grp'), may hold values from 0 to 32767, as said below
- clamp_values: float32 [1024, 4], P('grp'), may hold values from 2 to 8
Outputs:
- resid_out: bfloat16 [1024, 8192], P('grp', 'tp')
- features: bfloat16 [1024, 32768], P('tp', 'grp')
Inputs may be any that keep to these rules, and one draw needn't show every extreme that they name: Entries of kv_cache whose third index divided by 4 agrees are equal. `clamp_ids`: a row's 4 ids are (b + c * 8192) modulo 32768 for c = 0 .. 3.
All inputs are finite; a program needn't handle non-finite values. No bound on the sum of `lengths` on one device may be relied on, other than what follows from the above.
Results may differ from a plain program's by a relative error of at most 0.008.
Values may be sent and summed in bfloat16 or wider, within the bound.
No kernel may reach another device: no remote copies, remote signals or barrier semaphores. Data moves between devices by JAX's collectives and lax.ppermute only.
A program may use at most 128 MiB of HBM per device.

v0:
```python
import jax
import jax.numpy as jnp
from jax import lax
from jax.sharding import PartitionSpec as P

HEAD_DIM = 128
KV_HEADS = 4


def clamp_delta(latent_block, id_table, value_table, offset):
    width = latent_block.shape[1]
    columns = jnp.arange(width, dtype=jnp.int32)
    local_ids = id_table - offset
    current = latent_block.astype(jnp.float32)
    delta_total = jnp.zeros(latent_block.shape, jnp.float32)
    for slot_index in range(id_table.shape[1]):
        is_hit = columns[None, :] == local_ids[:, slot_index : slot_index + 1]
        clamped_now = jnp.sum(jnp.where(is_hit, current, 0.0), axis=1, keepdims=True)
        delta_total = delta_total + jnp.where(
            is_hit, value_table[:, slot_index : slot_index + 1] - clamped_now, 0.0
        )
    return delta_total.astype(jnp.bfloat16)


def per_device(
    resid_in,
    queries,
    kv_cache,
    new_kv,
    lengths,
    out_weight,
    enc_weight,
    enc_bias,
    dec_weight,
    clamp_ids,
    clamp_values,
):
    tp_count = lax.axis_size("tp")
    tp_rank = lax.axis_index("tp")
    grp_rank = lax.axis_index("grp")
    row_count = resid_in.shape[0]
    own_heads = queries.shape[1] // HEAD_DIM
    slot_count = kv_cache.shape[3]
    score_scale = HEAD_DIM ** (-0.5)
    query_heads = queries.reshape(row_count, own_heads, HEAD_DIM)
    cache_keys = kv_cache[0, :, 0]
    cache_values = kv_cache[1, :, 0]
    kv_index = tp_rank // (tp_count // KV_HEADS)
    new_key = lax.dynamic_index_in_dim(new_kv[0], kv_index, 1, keepdims=False)
    new_value = lax.dynamic_index_in_dim(new_kv[1], kv_index, 1, keepdims=False)
    scores = (
        jnp.einsum("shd,spd->shp", query_heads, cache_keys, preferred_element_type=jnp.float32)
        * score_scale
    )
    new_score = (
        jnp.einsum("shd,sd->sh", query_heads, new_key, preferred_element_type=jnp.float32)
        * score_scale
    )
    slot_index = jnp.arange(slot_count, dtype=jnp.int32)
    is_valid = (slot_index[None, :] < lengths[:, None])[:, None, :]
    top_score = jnp.maximum(jnp.max(jnp.where(is_valid, scores, -jnp.inf), axis=-1), new_score)
    prob_cache = jnp.where(is_valid, jnp.exp(scores - top_score[..., None]), 0.0)
    new_prob = jnp.exp(new_score - top_score)
    total_weight = jnp.sum(prob_cache, axis=-1) + new_prob
    new_rounded = lax.optimization_barrier(new_prob.astype(jnp.bfloat16)).astype(jnp.float32)
    weighted = jnp.einsum(
        "shp,spd->shd",
        prob_cache.astype(jnp.bfloat16),
        cache_values,
        preferred_element_type=jnp.float32,
    )
    weighted = weighted + new_rounded[..., None] * new_value.astype(jnp.float32)[:, None, :]
    head_output = (
        (weighted / total_weight[..., None])
        .astype(jnp.bfloat16)
        .reshape(row_count, own_heads * HEAD_DIM)
    )
    attn_part = jnp.dot(head_output, out_weight, preferred_element_type=jnp.float32)
    attn_cols = lax.psum_scatter(attn_part, "tp", scatter_dimension=1, tiled=True)
    resid_mid = (resid_in.astype(jnp.float32) + attn_cols).astype(jnp.bfloat16)
    id_table, value_table = (
        lax.all_gather(clamp_ids, "grp", axis=0, tiled=True),
        lax.all_gather(clamp_values, "grp", axis=0, tiled=True),
    )
    pre_part = jnp.dot(
        lax.all_gather(resid_mid, "grp", axis=0, tiled=True),
        enc_weight,
        preferred_element_type=jnp.float32,
    )
    all_rows = pre_part.shape[0]
    lat_span = enc_weight.shape[1]
    span_start = grp_rank * lat_span
    pre_act = lax.psum(pre_part, "tp")
    latent_block = jnp.maximum(pre_act + enc_bias, 0.0).astype(jnp.bfloat16)
    out_rows = all_rows // tp_count
    feature_out = lax.dynamic_slice_in_dim(latent_block, tp_rank * out_rows, out_rows, 0)
    delta_lat = clamp_delta(latent_block, id_table, value_table, span_start)
    edit_part = jnp.dot(delta_lat, dec_weight, preferred_element_type=jnp.float32)
    edit_whole = lax.psum(edit_part, "grp")
    edit_mine = lax.dynamic_slice_in_dim(edit_whole, grp_rank * row_count, row_count, 0)
    resid_out = (resid_mid.astype(jnp.float32) + edit_mine).astype(jnp.bfloat16)
    return (resid_out, feature_out)


def solution(mesh):
    placed = (
        P("grp", "tp"),
        P("grp", "tp"),
        P(None, "grp", "tp", None, None),
        P(None, "grp", None, None),
        P("grp"),
        P("tp", None),
        P("tp", "grp"),
        P("grp"),
        P("grp", "tp"),
        P("grp", None),
        P("grp", None),
    )
    return jax.shard_map(
        per_device,
        mesh=mesh,
        in_specs=placed,
        out_specs=(P("grp", "tp"), P("tp", "grp")),
        check_vma=False,
    )
```

profile of v0, /device:TPU:8, one launch (start us, length us, event | category | flops | bytes accessed | tf_op | source)
XLA Modules:
  0.0 511.2 jit_solution(2312959779147829518)
XLA Ops:
  7.2 0.0 copy-start
  7.2 0.0 copy-start.3
  7.2 0.0 reduce-scatter.2.cloned.1.call-start
  7.3 1.1 fusion.30
  8.3 0.1 dynamic-slice_convert_fusion
  8.4 0.8 reshape.42
  9.2 0.0 copy-start.1
  9.2 0.9 iota_compare_fusion.4
  10.1 0.2 fusion.24
  10.3 3.0 select_reduce_fusion
  13.3 0.2 fusion.29
  13.6 2.3 fusion.19
  15.9 0.0 copy-done.1
  15.9 2.2 fusion.20
  18.1 0.0 reduce-scatter.2.cloned.1.call-update
  18.1 0.0 all-gather.4.cloned.1.call-start
  18.2 65.8 %reduce-scatter.2.cloned.1.call-done = f32[64,512]{1,0:T(8,128)} async-done(((f32[64,8192]{1,0:T(8,128)}), f32[64,512]{1,0:T(8,128)}) %reduce-scatter.2.cloned.1.call-update) | async-done | bytes 131088 | tf_op jit(solution)/shard_map/reduce_scatter | solution.py:79
  84.0 0.0 copy-done.3
  84.0 1.5 add_convert_fusion.3
  85.6 0.0 all-gather.4.cloned.1.call-update
  85.6 0.0 copy-start.5
  85.6 0.0 copy-start.6
  85.6 0.0 copy-start.4
  85.6 0.0 all-reduce.3.cloned.1.call-start
  85.7 82.6 %all-gather.4.cloned.1.call-done = bf16[1024,512]{1,0:T(8,128)(2,1)} async-done(((bf16[64,512]{1,0:T(8,128)(2,1)}), bf16[1024,512]{1,0:T(8,128)(2,1)}) %all-gather.4.cloned.1.call-update) | async-done | bytes 1048592 | tf_op jit(solution)/shard_map/all_gather | solution.py:86
  168.2 0.0 copy-done
  168.2 6.8 %fusion.32 = f32[1024,2048]{1,0:T(8,128)} fusion(bf16[1024,512]{1,0:T(8,128)(2,1)} %all-gather.4.cloned.1.call-done, bf16[512,2048]{1,0:T(8,128)(2,1)S(1)} %copy-done), kind=kOutput, calls=%fused_computation.60 | convolution fusion | flops 2147483648 | bytes 11534336 | tf_op jit(solution)/shard_map/dot_general | solution.py:85
  175.0 0.0 all-reduce.3.cloned.1.call-update
  175.0 0.0 all-reduce.5.cloned.1.call-start
  175.1 0.0 copy-done.5
  175.1 37.5 %all-gather = s32[16,64,4]{1,2,0:T(4,128)S(1)} all-gather(s32[1,64,4]{1,2,0:T(4,128)S(1)} %bitcast.75), channel_id=1, replica_groups=mesh['tp'=16,'grp'=16] {'grp'}, dimensions={0}, use_global_device_ids=true | all-gather | bytes 17408 | tf_op jit(solution)/shard_map/all_gather | solution.py:82
  212.6 0.1 reshape.50
  212.7 0.0 copy-done.6
  212.7 37.4 %all-gather.1 = f32[16,64,4]{1,2,0:T(4,128)S(1)} all-gather(f32[1,64,4]{1,2,0:T(4,128)S(1)} %bitcast.76), channel_id=1, replica_groups=mesh['tp'=16,'grp'=16] {'grp'}, dimensions={0}, use_global_device_ids=true | all-gather | bytes 17408 | tf_op jit(solution)/shard_map/all_gather | solution.py:83
  250.1 0.1 reshape.48
  250.2 66.4 %all-reduce.3.cloned.1.call-done = f32[1024,2048]{1,0:T(8,128)} async-done(((f32[1024,2048]{1,0:T(8,128)}), f32[1024,2048]{1,0:T(8,128)}) %all-reduce.3.cloned.1.call-update) | async-done | bytes 8388624 | tf_op jit(solution)/shard_map/psum | solution.py:93
  316.6 0.0 copy-start.7
  316.6 0.0 copy-done.4
  316.6 9.0 %fusion = (f32[1024]{0:T(1024)S(1)}, f32[1024]{0:T(1024)S(1)}, f32[1024]{0:T(1024)S(1)}, f32[1024]{0:T(1024)S(1)}, bf16[1024,2048]{1,0:T(8,128)(2,1)}) fusion(s32[1024]{0:T(1024)S(1)} %bitcast.68, s32[1024]{0:T(1024)S(1)} %bitcast.66, s32[1024]{0:T(1024)S(1)} %bitcast.64, s32[1024]{0:T(1024)S(1)} %bitcast.62, f32[1024,2048]{1,0:T(8,128)} %all-reduce.3.cloned.1.call-done, ...), kind=kLoop, calls=%fused_computation.4 | loop fusion | flops 33550336 | bytes 12623872 | tf_op jit(solution)/shard_map/reduce_sum | solution.py:18
  325.6 0.0 copy-done.7
  325.6 0.0 copy-start.2
  325.6 6.1 %fusion.4 = f32[1024,512]{1,0:T(8,128)} fusion(bf16[2048,512]{1,0:T(8,128)(2,1)S(1)} %copy-done.7, f32[1024]{0:T(1024)S(1)} %bitcast.72, s32[1024]{0:T(1024)S(1)} %bitcast.63, f32[1024]{0:T(1024)S(1)} %bitcast.73, s32[1024]{0:T(1024)S(1)} %bitcast.65, f32[1024]{0:T(1024)S(1)} %bitcast.74, s32[1024]{0:T(1024)S(1)} %bitcast.67, f32[1024]{0:T(1024)S(1)} %bitcast.71, ...), kind=kOutput, calls=%fused_computation.14 | convolution fusion | flops 2172649472 | bytes 4227072 | tf_op jit(solution)/shard_map/dot_general | solution.py:98
  331.7 0.0 all-reduce.5.cloned.1.call-update
  331.7 1.7 constant_dynamic-slice_fusion
  333.4 169.7 %all-reduce.5.cloned.1.call-done = f32[1024,512]{1,0:T(8,128)} async-done(((f32[1024,512]{1,0:T(8,128)}), f32[1024,512]{1,0:T(8,128)}) %all-reduce.5.cloned.1.call-update) | async-done | bytes 2097168 | tf_op jit(solution)/shard_map/psum | solution.py:99
  503.1 0.0 copy-done.2
  503.1 1.5 add_convert_fusion.2
  (8 shorter events, 0.1 us)
Async XLA Ops:
  7.2 161.1 %copy-start = (bf16[512,2048]{1,0:T(8,128)(2,1)S(1)}, bf16[512,2048]{1,0:T(8,128)(2,1)}, u32[]{:S(2)}) copy-start(bf16[512,2048]{1,0:T(8,128)(2,1)} %param.17) | copy-start | bytes 6291460
  7.2 76.8 %copy-start.3 = (bf16[64,512]{1,0:T(8,128)(2,1)S(1)}, bf16[64,512]{1,0:T(8,128)(2,1)}, u32[]{:S(2)}) copy-start(bf16[64,512]{1,0:T(8,128)(2,1)} %param.11) | copy-start | bytes 196612
  7.2 76.8 %reduce-scatter.2.cloned.1.call-start = ((), (), s32[]{:S(2)}) async-start(), calls=%async_computation.1 | async-start | bytes 2228224 | tf_op jit(solution)/shard_map/reduce_scatter | solution.py:79
  9.2 6.7 %copy-start.1 = (bf16[256,8192]{1,0:T(8,128)(2,1)S(1)}, bf16[256,8192]{1,0:T(8,128)(2,1)}, u32[]{:S(2)}) copy-start(bf16[256,8192]{1,0:T(8,128)(2,1)} %param.16) | copy-start | bytes 12582916
  18.1 150.1 %all-gather.4.cloned.1.call-start = ((), (), s32[]{:S(2)}) async-start(), calls=%async_computation.2 | async-start | bytes 1114112 | tf_op jit(solution)/shard_map/all_gather | solution.py:86
  85.6 89.5 %copy-start.5 = (s32[64,4]{0,1:T(4,128)S(1)}, s32[64,4]{0,1:T(4,128)}, u32[]{:S(2)}) copy-start(s32[64,4]{0,1:T(4,128)} %param.20) | copy-start | bytes 3076
  85.6 127.1 %copy-start.6 = (f32[64,4]{0,1:T(4,128)S(1)}, f32[64,4]{0,1:T(4,128)}, u32[]{:S(2)}) copy-start(f32[64,4]{0,1:T(4,128)} %param.21) | copy-start | bytes 3076
  85.6 231.0 %copy-start.4 = (f32[2048]{0:T(1024)S(1)}, f32[2048]{0:T(1024)}, u32[]{:S(2)}) copy-start(f32[2048]{0:T(1024)} %param.18) | copy-start | bytes 24580
  85.6 231.0 %all-reduce.3.cloned.1.call-start = ((), (), s32[]{:S(2)}) async-start(), calls=%async_computation.3 | async-start | bytes 16777216 | tf_op jit(solution)/shard_map/psum | solution.py:93
  175.0 328.0 %all-reduce.5.cloned.1.call-start = ((), (), s32[]{:S(2)}) async-start(), calls=%async_computation.4 | async-start | bytes 4194304 | tf_op jit(solution)/shard_map/psum | solution.py:99
  316.6 9.0 %copy-start.7 = (bf16[2048,512]{1,0:T(8,128)(2,1)S(1)}, bf16[2048,512]{1,0:T(8,128)(2,1)}, u32[]{:S(2)}) copy-start(bf16[2048,512]{1,0:T(8,128)(2,1)} %param.19) | copy-start | bytes 6291460
  325.6 177.5 %copy-start.2 = (bf16[64,512]{1,0:T(8,128)(2,1)S(1)}, bf16[64,512]{1,0:T(8,128)(2,1)}, u32[]{:S(2)}) copy-start(bf16[64,512]{1,0:T(8,128)(2,1)} %add_convert_fusion.3) | copy-start | bytes 196612
Sparse Core Ops, SparseCore 0:
  18.3 65.6 reduce-scatter.1
  87.2 81.0 all-gather.3
  175.2 141.4 all-reduce.2
  331.9 171.1 all-reduce.4
where the time goes:
time: 512 us; the launch traced here: 511 us
  waiting for transfers between devices  385 us (75%)
  blocking collectives  74.9 us (15%)
  matrix products  20.6 us (4%)
  between operations  13.9 us (3%)
  other arithmetic  13.3 us (3%)
    psum x1, waiting for transfers between devices, per_device(): edit_whole = lax.psum(edit_part, 'grp')  170 us
    all_gather x1, waiting for transfers between devices, per_device(): lax.all_gather(resid_mid, 'grp', axis=0, tiled=True)  82.6 us
    psum x1, waiting for transfers between devices, per_device(): pre_act = lax.psum(pre_part, 'tp')  66.4 us
    reduce_scatter x1, waiting for transfers between devices, per_device(): lax.psum_scatter(attn_part, 'tp', scatter_dimension=1, tiled=True)  65.8 us
    all_gather x1, blocking collectives, per_device(): lax.all_gather(clamp_ids, 'grp', axis=0, tiled=True)  37.5 us
    all_gather x1, blocking collectives, per_device(): lax.all_gather(clamp_values, 'grp', axis=0, tiled=True)  37.4 us
  transfers between devices with their start and end apart: 4, of which 4 were waited for; matrix products, arithmetic and copies ran while one was open for 0% of the time, Pallas kernels for 0%

commit v1 on v0

--- a/solution.py
+++ b/solution.py
@@ -2,9 +2,15 @@
 import jax.numpy as jnp
 from jax import lax
 from jax.sharding import PartitionSpec as P
+from jax.lax import all_to_all, axis_size
 
 HEAD_DIM = 128
 KV_HEADS = 4
+
+
+def handle_the_local_data(xx, mesh_name="grp"):
+    state_next = all_to_all(jnp.stack([xx for _ in range(axis_size(mesh_name))]), mesh_name, 0, 0)
+    return jnp.concatenate(state_next, 0)
 
 
 def clamp_delta(latent_block, id_table, value_table, offset):
@@ -80,7 +86,7 @@
     resid_mid = (resid_in.astype(jnp.float32) + attn_cols).astype(jnp.bfloat16)
     id_table, value_table = (
         lax.all_gather(clamp_ids, "grp", axis=0, tiled=True),
-        lax.all_gather(clamp_values, "grp", axis=0, tiled=True),
+        handle_the_local_data(clamp_values),
     )
     pre_part = jnp.dot(
         lax.all_gather(resid_mid, "grp", axis=0, tiled=True),

time: 512 us -> 511 us (level)
  blocking collectives: 74.9 us -> 41.2 us
  waiting for transfers between devices: 385 us -> 412 us
    all_gather x1 -> x0, blocking collectives: 37.4 us -> none  [per_device(): lax.all_gather(clamp_values, 'grp', axis=0, tiled=True)]
    psum x1, waiting for transfers between devices: 66.4 us -> 93.4 us  [per_device(): pre_act = lax.psum(pre_part, 'tp')]
  transfers between devices with their start and end apart: 4 -> 5, of which waited for: 4 -> 4; matrix products, arithmetic and copies ran while one was open for 0% -> 1% of each run, Pallas kernels for 0% -> 0%
where the time goes in v1:
time: 511 us
  waiting for transfers between devices  412 us (81%)
  blocking collectives  41.2 us (8%)
  matrix products  20.6 us (4%)
  other arithmetic  14 us (3%)
  between operations  14 us (3%)
    psum x1, waiting for transfers between devices, per_device(): edit_whole = lax.psum(edit_part, 'grp')  170 us
    psum x1, waiting for transfers between devices, per_device(): pre_act = lax.psum(pre_part, 'tp')  93.4 us
    all_gather x1, waiting for transfers between devices, per_device(): lax.all_gather(resid_mid, 'grp', axis=0, tiled=True)  82.6 us
    reduce_scatter x1, waiting for transfers between devices, per_device(): lax.psum_scatter(attn_part, 'tp', scatter_dimension=1, tiled=True)  65.8 us
    all_gather x1, blocking collectives, per_device(): lax.all_gather(clamp_ids, 'grp', axis=0, tiled=True)  41.2 us
  transfers between devices with their start and end apart: 5, of which 4 were waited for; matrix products, arithmetic and copies ran while one was open for 1% of the time, Pallas kernels for 0%

profile of v1, /device:TPU:8, one launch (start us, length us, event | category | flops | bytes accessed | tf_op | source)
XLA Modules:
  0.0 510.6 jit_solution(12093215585327898740)
XLA Ops:
  7.2 0.0 copy-start
  7.2 0.0 copy-start.3
  7.2 0.0 reduce-scatter.2.cloned.1.call-start
  7.3 1.1 fusion.30
  8.3 0.1 dynamic-slice_convert_fusion
  8.4 0.8 reshape.47
  9.2 0.0 copy-start.1
  9.2 0.9 iota_compare_fusion.4
  10.1 0.2 fusion.24
  10.3 3.0 select_reduce_fusion
  13.3 0.2 fusion.29
  13.6 2.3 fusion.19
  15.9 0.0 copy-done.1
  15.9 2.2 fusion.20
  18.1 0.0 reduce-scatter.2.cloned.1.call-update
  18.2 0.0 all-gather.3.cloned.1.call-start
  18.2 65.8 %reduce-scatter.2.cloned.1.call-done = f32[64,512]{1,0:T(8,128)} async-done(((f32[64,8192]{1,0:T(8,128)}), f32[64,512]{1,0:T(8,128)}) %reduce-scatter.2.cloned.1.call-update) | async-done | bytes 131088 | tf_op jit(solution)/shard_map/reduce_scatter | solution.py:85
  84.0 0.0 copy-done.3
  84.0 1.5 add_convert_fusion.3
  85.5 0.0 all-gather.3.cloned.1.call-update
  85.6 0.0 copy-start.5
  85.6 0.0 copy-start.6
  85.6 0.0 copy-start.4
  85.6 0.0 all-reduce.3.cloned.1.call-start
  85.6 82.6 %all-gather.3.cloned.1.call-done = bf16[1024,512]{1,0:T(8,128)(2,1)} async-done(((bf16[64,512]{1,0:T(8,128)(2,1)}), bf16[1024,512]{1,0:T(8,128)(2,1)}) %all-gather.3.cloned.1.call-update) | async-done | bytes 1048592 | tf_op jit(solution)/shard_map/all_gather | solution.py:92
  168.2 6.8 %fusion.32 = f32[1024,2048]{1,0:T(8,128)} fusion(bf16[1024,512]{1,0:T(8,128)(2,1)} %all-gather.3.cloned.1.call-done, bf16[512,2048]{1,0:T(8,128)(2,1)S(1)} %copy-done), kind=kOutput, calls=%fused_computation.61 | convolution fusion | flops 2147483648 | bytes 11534336 | tf_op jit(solution)/shard_map/dot_general | solution.py:91
  175.0 0.0 all-reduce.3.cloned.1.call-update
  175.1 0.7 reshape.57
  175.8 4.1 all-to-all-start
  179.9 0.0 all-reduce.5.cloned.1.call-start
  179.9 0.0 copy-done.6
  180.0 41.2 %all-gather = s32[16,64,4]{1,2,0:T(4,128)S(1)} all-gather(s32[1,64,4]{1,2,0:T(4,128)S(1)} %bitcast.78), channel_id=1, replica_groups=mesh['tp'=16,'grp'=16] {'grp'}, dimensions={0}, use_global_device_ids=true | all-gather | bytes 17408 | tf_op jit(solution)/shard_map/all_gather | solution.py:88
  221.2 0.1 reshape.54
  221.3 0.0 all-to-all-done
  221.3 0.5 broadcast.19
  221.8 0.7 reduce
  222.5 0.1 reshape.58
  222.6 0.1 reshape.49
  222.7 93.4 %all-reduce.3.cloned.1.call-done = f32[1024,2048]{1,0:T(8,128)} async-done(((f32[1024,2048]{1,0:T(8,128)}), f32[1024,2048]{1,0:T(8,128)}) %all-reduce.3.cloned.1.call-update) | async-done | bytes 8388624 | tf_op jit(solution)/shard_map/psum | solution.py:99
  316.1 9.0 %fusion = (f32[1024]{0:T(1024)S(1)}, f32[1024]{0:T(1024)S(1)}, f32[1024]{0:T(1024)S(1)}, f32[1024]{0:T(1024)S(1)}, bf16[1024,2048]{1,0:T(8,128)(2,1)}) fusion(s32[1024]{0:T(1024)S(1)} %bitcast.71, s32[1024]{0:T(1024)S(1)} %bitcast.69, s32[1024]{0:T(1024)S(1)} %bitcast.67, s32[1024]{0:T(1024)S(1)} %bitcast.65, f32[1024,2048]{1,0:T(8,128)} %all-reduce.3.cloned.1.call-done, ...), kind=kLoop, calls=%fused_computation.4 | loop fusion | flops 33550336 | bytes 12623872 | tf_op jit(solution)/shard_map/reduce_sum | solution.py:24
  325.0 0.0 copy-done.7
  325.1 0.0 copy-start.2
  325.1 6.1 %fusion.4 = f32[1024,512]{1,0:T(8,128)} fusion(bf16[2048,512]{1,0:T(8,128)(2,1)S(1)} %copy-done.7, f32[1024]{0:T(1024)S(1)} %bitcast.75, s32[1024]{0:T(1024)S(1)} %bitcast.66, f32[1024]{0:T(1024)S(1)} %bitcast.76, s32[1024]{0:T(1024)S(1)} %bitcast.68, f32[1024]{0:T(1024)S(1)} %bitcast.77, s32[1024]{0:T(1024)S(1)} %bitcast.70, f32[1024]{0:T(1024)S(1)} %bitcast.74, ...), kind=kOutput, calls=%fused_computation.14 | convolution fusion | flops 2172649472 | bytes 4227072 | tf_op jit(solution)/shard_map/dot_general | solution.py:104
  331.2 0.0 all-reduce.5.cloned.1.call-update
  331.2 1.7 constant_dynamic-slice_fusion
  332.9 169.7 %all-reduce.5.cloned.1.call-done = f32[1024,512]{1,0:T(8,128)} async-done(((f32[1024,512]{1,0:T(8,128)}), f32[1024,512]{1,0:T(8,128)}) %all-reduce.5.cloned.1.call-update) | async-done | bytes 2097168 | tf_op jit(solution)/shard_map/psum | solution.py:105
  502.6 0.0 copy-done.2
  502.6 1.5 add_convert_fusion.2
  (13 shorter events, 0.1 us)
Async XLA Ops:
  7.2 161.1 %copy-start = (bf16[512,2048]{1,0:T(8,128)(2,1)S(1)}, bf16[512,2048]{1,0:T(8,128)(2,1)}, u32[]{:S(2)}) copy-start(bf16[512,2048]{1,0:T(8,128)(2,1)} %param.17) | copy-start | bytes 6291460
  7.2 76.8 %copy-start.3 = (bf16[64,512]{1,0:T(8,128)(2,1)S(1)}, bf16[64,512]{1,0:T(8,128)(2,1)}, u32[]{:S(2)}) copy-start(bf16[64,512]{1,0:T(8,128)(2,1)} %param.11) | copy-start | bytes 196612
  7.2 76.8 %reduce-scatter.2.cloned.1.call-start = ((), (), s32[]{:S(2)}) async-start(), calls=%async_computation.2 | async-start | bytes 2228224 | tf_op jit(solution)/shard_map/reduce_scatter | solution.py:85
  9.2 6.7 %copy-start.1 = (bf16[256,8192]{1,0:T(8,128)(2,1)S(1)}, bf16[256,8192]{1,0:T(8,128)(2,1)}, u32[]{:S(2)}) copy-start(bf16[256,8192]{1,0:T(8,128)(2,1)} %param.16) | copy-start | bytes 12582916
  18.2 150.1 %all-gather.3.cloned.1.call-start = ((), (), s32[]{:S(2)}) async-start(), calls=%async_computation.3 | async-start | bytes 1114112 | tf_op jit(solution)/shard_map/all_gather | solution.py:92
  85.6 89.5 %copy-start.5 = (f32[64,4]{0,1:T(4,128)S(1)}, f32[64,4]{0,1:T(4,128)}, u32[]{:S(2)}) copy-start(f32[64,4]{0,1:T(4,128)} %param.21) | copy-start | bytes 3076
  85.6 94.4 %copy-start.6 = (s32[64,4]{0,1:T(4,128)S(1)}, s32[64,4]{0,1:T(4,128)}, u32[]{:S(2)}) copy-start(s32[64,4]{0,1:T(4,128)} %param.20) | copy-start | bytes 3076
  85.6 230.5 %copy-start.4 = (f32[2048]{0:T(1024)S(1)}, f32[2048]{0:T(1024)}, u32[]{:S(2)}) copy-start(f32[2048]{0:T(1024)} %param.18) | copy-start | bytes 24580
  85.6 230.5 %all-reduce.3.cloned.1.call-start = ((), (), s32[]{:S(2)}) async-start(), calls=%async_computation.4 | async-start | bytes 16777216 | tf_op jit(solution)/shard_map/psum | solution.py:99
  175.8 45.5 %all-to-all-start = ((f32[16,1,256]{2,1,0:T(1,128)}), f32[16,1,256]{2,1,0:T(1,128)S(1)}, u32[]{:S(2)}, u32[]{:S(2)}) async-start(f32[16,1,256]{2,1,0:T(1,128)} %reshape.57), calls=%async_computation.1 | async-start | bytes 32768 | tf_op jit(solution)/shard_map/all_to_all | solution.py:12
  179.9 322.7 %all-reduce.5.cloned.1.call-start = ((), (), s32[]{:S(2)}) async-start(), calls=%async_computation.5 | async-start | bytes 4194304 | tf_op jit(solution)/shard_map/psum | solution.py:105
  316.1 9.0 %copy-start.7 = (bf16[2048,512]{1,0:T(8,128)(2,1)S(1)}, bf16[2048,512]{1,0:T(8,128)(2,1)}, u32[]{:S(2)}) copy-start(bf16[2048,512]{1,0:T(8,128)(2,1)} %param.19) | copy-start | bytes 6291460
  325.1 177.5 %copy-start.2 = (bf16[64,512]{1,0:T(8,128)(2,1)S(1)}, bf16[64,512]{1,0:T(8,128)(2,1)}, u32[]{:S(2)}) copy-start(bf16[64,512]{1,0:T(8,128)(2,1)} %add_convert_fusion.3) | copy-start | bytes 196612
Sparse Core Ops, SparseCore 0:
  18.3 65.6 reduce-scatter.1
  87.1 81.0 all-gather.2
  175.2 140.8 all-reduce.2
  331.3 171.2 all-reduce.4
